TPU v7x, 128 devices: a whole 4x4x4 slice. The times are simulated.
128 devices in a mesh: space: 8 (over z, x_hi), ens: 16 (over y, x_lo, core).
Axes of the slice: x: 4 (x_hi: 2, x_lo: 2; x = x_hi * 2 + x_lo), y: 4, z: 4, core: 2. Of those that a mesh axis runs over, the one named last changes fastest.
Arguments:
- log_perm: float32 [128, 16, 64, 512], P('ens', 'space'), may hold values from -4 to 4
- storage: float32 [16, 64, 512], P('space'), may hold values from 0.5 to 2
- head_init: float32 [16, 64, 512], P('space'), may hold values from -6 to 6
- well_cells: int32 [16], replicated, may hold values from 0 to 524287
- well_rates: float32 [16], replicated, may hold values from -12 to 12
- obs_cells: int32 [32], replicated, may hold values from 0 to 524287
- obs_values: float32 [32], replicated, may hold values from -6 to 6
- noise_var: float32 [32], replicated, may hold values from 0.05 to 0.5
- step_size: float32 [1], replicated, may hold values from 0.5 to 2
- perturb: float32 [128, 32], P('ens'), may hold values from -2 to 2
Outputs:
- head_field: float32 [128, 16, 64, 512], P('ens', 'space')
- updated: float32 [128, 16, 64, 512], P('ens', 'space')
All inputs are finite; a program needn't handle non-finite values.
Results may differ from a plain program's by a relative error of at most 0.00025.
Values sent between devices are 32-bit elements; how exact they have to be, the bound alone decides.
A program may use at most 192 MiB of HBM per device.

v0:
```python
import jax
import jax.numpy as jnp
from jax import lax
from jax.sharding import PartitionSpec as P

SWEEPS = 3
OMEGA = 0.8
HIGHEST = lax.Precision.HIGHEST
DIRECTIONS = [
    (a, b, c) for a in (-1, 0, 1) for b in (-1, 0, 1) for c in (-1, 0, 1) if (a, b, c) != (0, 0, 0)
]


def padded_2(block, sides, width):
    for axis, dim in sides:
        count = lax.axis_size(axis)
        forward = [(i, i + 1) for i in range(count - 1)]
        backward = [(target, source) for source, target in forward]
        low = lax.ppermute(
            lax.slice_in_dim(block, block.shape[dim] - width, None, axis=dim), axis, forward
        )
        high = lax.ppermute(lax.slice_in_dim(block, 0, width, axis=dim), axis, backward)
        block = jnp.concatenate([low, block, high], axis=dim)
    return block


def shifted(padded, a, b, c, planes, depth, across):
    return padded[..., 1 + a : 1 + a + planes, 1 + b : 1 + b + depth, 1 + c : 1 + c + across]


def solve_pair(factor, residual):
    first = lax.linalg.triangular_solve(factor, residual.T, left_side=True, lower=True)
    second = lax.linalg.triangular_solve(
        factor, first, left_side=True, lower=True, transpose_a=True
    )
    return second.T


def shards(
    log_perm,
    storage,
    head_init,
    well_cells,
    well_rates,
    obs_cells,
    obs_values,
    noise_var,
    step_size,
    perturb,
):
    members, planes, depth, across = log_perm.shape
    cell_count = planes * depth * across
    total_members = members * lax.axis_size("ens")
    offset = lax.axis_index("space") * cell_count
    cell_ids = lax.broadcasted_iota(jnp.int32, (1, cell_count), 1)
    hits = (cell_ids == (well_cells - offset)[:, None]).astype(jnp.float32)
    source = jnp.dot(well_rates, hits, precision=HIGHEST).reshape(planes, depth, across)
    permeability = jnp.exp(log_perm)
    rimmed = padded_2(permeability, (("space", 1),), 1)
    padded = jnp.pad(rimmed, ((0, 0), (0, 0), (1, 1), (1, 1)))
    transmit = []
    for a, b, c in DIRECTIONS:
        factor = 2.0 ** (1 - abs(a) - abs(b) - abs(c))
        neighbour = shifted(padded, a, b, c, planes, depth, across)
        transmit.append(factor * 2.0 * permeability * neighbour / (permeability + neighbour))
    diagonal = storage + sum(transmit)
    forcing = storage * head_init + source
    head_field = jnp.broadcast_to(head_init, log_perm.shape)
    for sweep_index in range(SWEEPS):
        rimmed_head = padded_2(head_field, (("space", 1),), 1)
        padded_head = jnp.pad(rimmed_head, ((0, 0), (0, 0), (1, 1), (1, 1)))
        gathered = sum(
            (
                transmit[i] * shifted(padded_head, a, b, c, planes, depth, across)
                for i, (a, b, c) in enumerate(DIRECTIONS)
            )
        )
        head_field = (1.0 - OMEGA) * head_field + OMEGA * (forcing + gathered) / diagonal
    local_obs = obs_cells - offset
    inside = ((local_obs >= 0) & (local_obs < cell_count)).astype(jnp.float32)
    picked = (
        jnp.take(
            head_field.reshape(members, cell_count), jnp.clip(local_obs, 0, cell_count - 1), axis=1
        )
        * inside
    )
    observed = lax.psum(picked, "space")
    every_obs = lax.all_gather(observed, "ens", axis=0, tiled=True)
    mean_obs = jnp.mean(every_obs, axis=0)
    spread = every_obs - mean_obs
    covariance = jnp.dot(spread.T, spread, precision=HIGHEST) / (total_members - 1)
    deviation = observed - mean_obs
    system = covariance + jnp.diag(noise_var / step_size[0])
    factor_lower = jnp.linalg.cholesky(system)
    gain_rows = solve_pair(factor_lower, obs_values[None, :] + perturb - observed)
    flat = log_perm.reshape(members, cell_count)
    piece_field = lax.all_gather(flat, "ens", axis=0, tiled=True)
    piece_dev = lax.all_gather(deviation, "ens", axis=0, tiled=True)
    mixing = jnp.dot(piece_dev, gain_rows.T, precision=HIGHEST)
    change = lax.dot_general(mixing, piece_field, (((0,), (0,)), ((), ())), precision=HIGHEST)
    updated = (flat + change / (total_members - 1)).reshape(log_perm.shape)
    return (head_field, updated)


def solution(mesh):
    return jax.shard_map(
        shards,
        mesh=mesh,
        in_specs=(
            P("ens", "space", None, None),
            P("space", None, None),
            P("space", None, None),
            P(),
            P(),
            P(),
            P(),
            P(),
            P(),
            P("ens", None),
        ),
        out_specs=(P("ens", "space", None, None), P("ens", "space", None, None)),
        check_vma=False,
    )
```

profile of v0, /device:TPU:1, one launch (start us, length us, event | category | flops | bytes accessed | tf_op | source)
XLA Modules:
  0.0 545.3 jit_solution(13911891176995488092)
XLA Ops:
  7.2 4.2 copy.30
  11.4 1.9 exp.3
  14.9 5.7 %collective-permute-start = (f32[8,1,64,512]{3,2,1,0:T(8,128)}, f32[8,1,64,512]{3,2,1,0:T(8,128)S(1)}, u32[]{:S(2)}, u32[]{:S(2)}) collective-permute-start(f32[8,1,64,512]{3,2,1,0:T(8,128)} %get-tuple-element.14), channel_id=1, source_target_pairs={{0,16},{16,32},{32,48},{48,64},{64,80},{80,96},{96,112},{1,17},{17... | collective-permute-start | bytes 3145736 | tf_op jit(solution)/shard_map/ppermute | solution.py:19
  23.1 6.5 %collective-permute-start.2 = (f32[8,1,64,512]{3,2,1,0:T(8,128)}, f32[8,1,64,512]{3,2,1,0:T(8,128)}, u32[]{:S(2)}, u32[]{:S(2)}) collective-permute-start(f32[8,1,64,512]{3,2,1,0:T(8,128)} %broadcast_in_dim.53), channel_id=1, source_target_pairs={{0,16},{16,32},{32,48},{48,64},{64,80},{80,96},{96,112},{1,17},{17... | collective-permute-start | bytes 3145736 | tf_op jit(solution)/shard_map/ppermute | solution.py:19
  32.1 2.1 fusion.4
  37.6 23.5 %collective-permute-done = f32[8,1,64,512]{3,2,1,0:T(8,128)S(1)} collective-permute-done((f32[8,1,64,512]{3,2,1,0:T(8,128)}, f32[8,1,64,512]{3,2,1,0:T(8,128)S(1)}, u32[]{:S(2)}, u32[]{:S(2)}) %collective-permute-start) | collective-permute-done | bytes 1048608 | tf_op jit(solution)/shard_map/ppermute | solution.py:19
  61.1 45.9 %collective-permute-done.1 = f32[8,1,64,512]{3,2,1,0:T(8,128)} collective-permute-done((f32[8,1,64,512]{3,2,1,0:T(8,128)}, f32[8,1,64,512]{3,2,1,0:T(8,128)}, u32[]{:S(2)}, u32[]{:S(2)}) %collective-permute-start.1) | collective-permute-done | bytes 1048608 | tf_op jit(solution)/shard_map/ppermute | solution.py:22
  107.0 3.7 select_maximum_fusion.6
  110.7 86.2 %collective-permute-done.3 = f32[8,1,64,512]{3,2,1,0:T(8,128)} collective-permute-done((f32[8,1,64,512]{3,2,1,0:T(8,128)}, f32[8,1,64,512]{3,2,1,0:T(8,128)}, u32[]{:S(2)}, u32[]{:S(2)}) %collective-permute-start.3) | collective-permute-done | bytes 1048608 | tf_op jit(solution)/shard_map/ppermute | solution.py:22
  197.2 4.7 select_maximum_fusion.4
  201.9 23.9 %fusion.71 = f32[8,2,64,512]{3,2,1,0:T(8,128)} fusion(f32[8,4,66,514]{3,2,1,0:T(8,128)S(1)} %select_maximum_fusion.4, f32[8,1,64,512]{3,2,1,0:T(8,128)} %collective-permute-done.3, f32[8,2,64,512]{3,2,1,0:T(8,128)} %copy-done.5, f32[8,1,64,512]{3,2,1,0:T(8,128)} %collective-permute-done.2, f32[2,64,512]{2,1,0:T(8,128)S(1)} %copy-done.7, ...), kind=kLoop, calls=%fused_computation.139 | loop fusion | flops 87031808 | bytes 114032640 | tf_op jit(solution)/shard_map/add | solution.py:78
  225.8 1.9 fusion.119
  227.7 6.2 %collective-permute-start.4 = (f32[8,1,64,512]{3,2,1,0:T(8,128)S(1)}, f32[8,1,64,512]{3,2,1,0:T(8,128)S(1)}, u32[]{:S(2)}, u32[]{:S(2)}) collective-permute-start(f32[8,1,64,512]{3,2,1,0:T(8,128)S(1)} %get-tuple-element.12), channel_id=1, source_target_pairs={{0,16},{16,32},{32,48},{48,64},{64,80},{80,96},{96,112},{1,17},{17... | collective-permute-start | bytes 3145736 | tf_op jit(solution)/shard_map/ppermute | solution.py:19
  235.5 16.8 %collective-permute-done.4 = f32[8,1,64,512]{3,2,1,0:T(8,128)S(1)} collective-permute-done((f32[8,1,64,512]{3,2,1,0:T(8,128)S(1)}, f32[8,1,64,512]{3,2,1,0:T(8,128)S(1)}, u32[]{:S(2)}, u32[]{:S(2)}) %collective-permute-start.4) | collective-permute-done | bytes 1048608 | tf_op jit(solution)/shard_map/ppermute | solution.py:19
  252.3 62.0 %collective-permute-done.5 = f32[8,1,64,512]{3,2,1,0:T(8,128)S(1)} collective-permute-done((f32[8,1,64,512]{3,2,1,0:T(8,128)S(1)}, f32[8,1,64,512]{3,2,1,0:T(8,128)S(1)}, u32[]{:S(2)}, u32[]{:S(2)}) %collective-permute-start.5) | collective-permute-done | bytes 1048608 | tf_op jit(solution)/shard_map/ppermute | solution.py:22
  315.2 2.7 select_maximum_fusion.2
  317.9 22.7 %fusion.40 = f32[8,2,64,512]{3,2,1,0:T(8,128)} fusion(f32[8,4,66,514]{3,2,1,0:T(8,128)S(1)} %select_maximum_fusion.2, f32[8,1,64,512]{3,2,1,0:T(8,128)} %copy-done.9, f32[8,2,64,512]{3,2,1,0:T(8,128)} %fusion.71, f32[8,1,64,512]{3,2,1,0:T(8,128)S(1)} %collective-permute-done.4, f32[2,64,512]{2,1,0:T(8,128)S(1)} %copy-done.7, ...), kind=kLoop, calls=%fused_computation.82 | loop fusion | flops 87556096 | bytes 113770496 | tf_op jit(solution)/shard_map/add | solution.py:78
  340.6 1.9 fusion.118
  342.5 4.7 collective-permute-start.6
  349.2 18.5 %collective-permute-done.6 = f32[8,1,64,512]{3,2,1,0:T(8,128)S(1)} collective-permute-done((f32[8,1,64,512]{3,2,1,0:T(8,128)S(1)}, f32[8,1,64,512]{3,2,1,0:T(8,128)S(1)}, u32[]{:S(2)}, u32[]{:S(2)}) %collective-permute-start.6) | collective-permute-done | bytes 1048608 | tf_op jit(solution)/shard_map/ppermute | solution.py:19
  367.7 25.0 %collective-permute-done.7 = f32[8,1,64,512]{3,2,1,0:T(8,128)S(1)} collective-permute-done((f32[8,1,64,512]{3,2,1,0:T(8,128)S(1)}, f32[8,1,64,512]{3,2,1,0:T(8,128)S(1)}, u32[]{:S(2)}, u32[]{:S(2)}) %collective-permute-start.7) | collective-permute-done | bytes 1048608 | tf_op jit(solution)/shard_map/ppermute | solution.py:22
  393.6 2.7 select_maximum_fusion
  396.3 22.7 %fusion.9 = f32[8,2,64,512]{3,2,1,0:T(8,128)} fusion(f32[8,4,66,514]{3,2,1,0:T(8,128)S(1)} %select_maximum_fusion, f32[8,1,64,512]{3,2,1,0:T(8,128)} %copy-done.8, f32[8,2,64,512]{3,2,1,0:T(8,128)} %fusion.40, f32[8,1,64,512]{3,2,1,0:T(8,128)S(1)} %collective-permute-done.6, f32[2,64,512]{2,1,0:T(8,128)S(1)} %copy-done.7, ...), kind=kLoop, calls=%fused_computation.25 | loop fusion | flops 87556096 | bytes 113770496 | tf_op jit(solution)/shard_map/add | solution.py:78
  419.0 18.0 %copy.24 = f32[8,2,64,512]{0,3,2,1:T(8,128)} copy(f32[8,2,64,512]{3,2,1,0:T(8,128)} %fusion.9) | data formatting | bytes 4194304 | tf_op jit(solution)/shard_map/add | solution.py:78
  437.0 11.1 %gather_fusion = f32[32,8]{1,0:T(8,128)S(1)} fusion(f32[8,65536]{0,1:T(8,128)} %bitcast.36, s32[1024]{0:T(1024)S(1)} %pad_clamp_fusion), kind=kCustom, calls=%fused_computation | custom fusion | bytes 2176 | tf_op jit(solution)/shard_map/jit(_take)/gather | solution.py:82
  448.2 18.1 %psum.7 = f32[8,32]{1,0:T(8,128)S(1)} all-reduce(f32[8,32]{1,0:T(8,128)S(1)} %multiply_bitcast_fusion), channel_id=1, replica_groups=mesh['space'=8,'ens'=16] {'space'}, use_global_device_ids=true, to_apply=%region_0.1 | all-reduce | flops 256 | bytes 2048 | tf_op jit(solution)/shard_map/psum | solution.py:87
  466.3 25.5 %all_gather.9 = f32[128,32]{1,0:T(8,128)S(1)} all-gather(f32[8,32]{1,0:T(8,128)S(1)} %psum.7), channel_id=1, replica_groups=mesh['space'=8,'ens'=16] {'ens'}, dimensions={0}, use_global_device_ids=true | all-gather | bytes 17408 | tf_op jit(solution)/shard_map/all_gather | solution.py:88
  492.3 2.9 cholesky.16
  496.6 2.4 custom-call.8
  499.0 16.7 %all_gather.10 = f32[128,32]{1,0:T(8,128)S(1)} all-gather(f32[8,32]{1,0:T(8,128)S(1)} %broadcast_subtract_fusion), channel_id=1, replica_groups=mesh['space'=8,'ens'=16] {'ens'}, dimensions={0}, use_global_device_ids=true | all-gather | bytes 17408 | tf_op jit(solution)/shard_map/all_gather | solution.py:98
  516.3 19.6 %fusion = f32[8,65536]{1,0:T(8,128)S(1)} fusion(f32[8,65536]{1,0:T(8,128)S(1)} %bitcast.38, f32[128,8]{0,1:T(8,128)S(1)} %fusion.121, f32[128,65536]{1,0:T(8,128)} %all-gather.2.cloned.1.call-done), kind=kOutput, calls=%fused_computation.2 | convolution fusion | flops 806354944 | bytes 37752832 | tf_op jit(solution)/shard_map/dot_general | solution.py:100
  535.9 2.5 copy.28
  (67 shorter events, 17.3 us)
Async XLA Ops:
  7.2 24.9 %copy-start = (f32[16]{0:T(128)S(1)}, f32[16]{0:T(128)}, u32[]{:S(2)}) copy-start(f32[16]{0:T(128)} %param.14) | copy-start | bytes 196
  7.2 509.1 %all-gather.2.cloned.1.call-start = ((), (), s32[]{:S(2)}) async-start(), calls=%async_computation | async-start | bytes 35651584 | tf_op jit(solution)/shard_map/all_gather | solution.py:97
  13.4 8.7 %copy-start.10 = (f32[2,64,512]{2,1,0:T(8,128)S(1)}, f32[2,64,512]{2,1,0:T(8,128)}, u32[]{:S(2)}) copy-start(f32[2,64,512]{2,1,0:T(8,128)} %param.12) | copy-start | bytes 786436
  14.9 17.1 %copy-start.15 = (s32[16]{0:T(128)S(1)}, s32[16]{0:T(128)}, u32[]{:S(2)}) copy-start(s32[16]{0:T(128)} %param.13) | copy-start | bytes 196
  14.9 46.2 %collective-permute-start = (f32[8,1,64,512]{3,2,1,0:T(8,128)}, f32[8,1,64,512]{3,2,1,0:T(8,128)S(1)}, u32[]{:S(2)}, u32[]{:S(2)}) collective-permute-start(f32[8,1,64,512]{3,2,1,0:T(8,128)} %get-tuple-element.14), channel_id=1, source_target_pairs={{0,16},{16,32},{32,48},{48,64},{64,80},{80,96},{96,112},{1,17},{17... | collective-permute-start | bytes 3145736 | tf_op jit(solution)/shard_map/ppermute | solution.py:19
  20.6 15.3 %copy-start.7 = (f32[2,64,512]{2,1,0:T(8,128)S(1)}, f32[2,64,512]{2,1,0:T(8,128)}, u32[]{:S(2)}) copy-start(f32[2,64,512]{2,1,0:T(8,128)} %param.11) | copy-start | bytes 786436
  20.6 86.4 %collective-permute-start.1 = (f32[8,1,64,512]{3,2,1,0:T(8,128)}, f32[8,1,64,512]{3,2,1,0:T(8,128)}, u32[]{:S(2)}, u32[]{:S(2)}) collective-permute-start(f32[8,1,64,512]{3,2,1,0:T(8,128)} %get-tuple-element.15), channel_id=1, source_target_pairs={{16,0},{32,16},{48,32},{64,48},{80,64},{96,80},{112,96},{17,1},{33... | collective-permute-start | bytes 3145736 | tf_op jit(solution)/shard_map/ppermute | solution.py:22
  23.1 87.6 %collective-permute-start.2 = (f32[8,1,64,512]{3,2,1,0:T(8,128)}, f32[8,1,64,512]{3,2,1,0:T(8,128)}, u32[]{:S(2)}, u32[]{:S(2)}) collective-permute-start(f32[8,1,64,512]{3,2,1,0:T(8,128)} %broadcast_in_dim.53), channel_id=1, source_target_pairs={{0,16},{16,32},{32,48},{48,64},{64,80},{80,96},{96,112},{1,17},{17... | collective-permute-start | bytes 3145736 | tf_op jit(solution)/shard_map/ppermute | solution.py:19
  30.7 166.1 %collective-permute-start.3 = (f32[8,1,64,512]{3,2,1,0:T(8,128)}, f32[8,1,64,512]{3,2,1,0:T(8,128)}, u32[]{:S(2)}, u32[]{:S(2)}) collective-permute-start(f32[8,1,64,512]{3,2,1,0:T(8,128)} %broadcast_in_dim.55), channel_id=1, source_target_pairs={{16,0},{32,16},{48,32},{64,48},{80,64},{96,80},{112,96},{17,1},{33... | collective-permute-start | bytes 3145736 | tf_op jit(solution)/shard_map/ppermute | solution.py:22
  37.6 159.3 %copy-start.11 = (f32[2,64,512]{2,1,0:T(8,128)S(1)}, f32[2,64,512]{2,1,0:T(8,128)}, u32[]{:S(2)}) copy-start(f32[2,64,512]{2,1,0:T(8,128)} %param.12) | copy-start | bytes 786436
  197.1 4.7 copy-start.5
  197.2 4.7 copy-start.2
  225.8 89.4 %copy-start.4 = (f32[8,2,64,512]{3,2,1,0:T(8,128)S(1)}, f32[8,2,64,512]{3,2,1,0:T(8,128)}, u32[]{:S(2)}) copy-start(f32[8,2,64,512]{3,2,1,0:T(8,128)} %fusion.71) | copy-start | bytes 6291460
  227.7 24.5 %collective-permute-start.4 = (f32[8,1,64,512]{3,2,1,0:T(8,128)S(1)}, f32[8,1,64,512]{3,2,1,0:T(8,128)S(1)}, u32[]{:S(2)}, u32[]{:S(2)}) collective-permute-start(f32[8,1,64,512]{3,2,1,0:T(8,128)S(1)} %get-tuple-element.12), channel_id=1, source_target_pairs={{0,16},{16,32},{32,48},{48,64},{64,80},{80,96},{96,112},{1,17},{17... | collective-permute-start | bytes 3145736 | tf_op jit(solution)/shard_map/ppermute | solution.py:19
  234.0 80.3 %collective-permute-start.5 = (f32[8,1,64,512]{3,2,1,0:T(8,128)S(1)}, f32[8,1,64,512]{3,2,1,0:T(8,128)S(1)}, u32[]{:S(2)}, u32[]{:S(2)}) collective-permute-start(f32[8,1,64,512]{3,2,1,0:T(8,128)S(1)} %get-tuple-element.13), channel_id=1, source_target_pairs={{16,0},{32,16},{48,32},{64,48},{80,64},{96,80},{112,96},{17,1},{33... | collective-permute-start | bytes 3145736 | tf_op jit(solution)/shard_map/ppermute | solution.py:22
  314.2 1.0 copy-start.9
  340.6 8.5 %copy-start.14 = (s32[32]{0:T(128)S(1)}, s32[32]{0:T(128)}, u32[]{:S(2)}) copy-start(s32[32]{0:T(128)} %param.15) | copy-start | bytes 388
  340.6 8.6 %copy-start.16 = (f32[32]{0:T(128)S(1)}, f32[32]{0:T(128)}, u32[]{:S(2)}) copy-start(f32[32]{0:T(128)} %param.17) | copy-start | bytes 388
  340.6 53.0 %copy-start.3 = (f32[8,2,64,512]{3,2,1,0:T(8,128)S(1)}, f32[8,2,64,512]{3,2,1,0:T(8,128)}, u32[]{:S(2)}) copy-start(f32[8,2,64,512]{3,2,1,0:T(8,128)} %fusion.40) | copy-start | bytes 6291460
  342.5 25.2 %collective-permute-start.6 = (f32[8,1,64,512]{3,2,1,0:T(8,128)S(1)}, f32[8,1,64,512]{3,2,1,0:T(8,128)S(1)}, u32[]{:S(2)}, u32[]{:S(2)}) collective-permute-start(f32[8,1,64,512]{3,2,1,0:T(8,128)S(1)} %get-tuple-element.10), channel_id=1, source_target_pairs={{0,16},{16,32},{32,48},{48,64},{64,80},{80,96},{96,112},{1,17},{17... | collective-permute-start | bytes 3145736 | tf_op jit(solution)/shard_map/ppermute | solution.py:19
  347.2 45.5 %collective-permute-start.7 = (f32[8,1,64,512]{3,2,1,0:T(8,128)S(1)}, f32[8,1,64,512]{3,2,1,0:T(8,128)S(1)}, u32[]{:S(2)}, u32[]{:S(2)}) collective-permute-start(f32[8,1,64,512]{3,2,1,0:T(8,128)S(1)} %get-tuple-element.11), channel_id=1, source_target_pairs={{16,0},{32,16},{48,32},{64,48},{80,64},{96,80},{112,96},{17,1},{33... | collective-permute-start | bytes 3145736 | tf_op jit(solution)/shard_map/ppermute | solution.py:22
  392.7 1.0 copy-start.8
  419.0 96.8 %copy-start.12 = (f32[8,32]{1,0:T(8,128)S(1)}, f32[8,32]{1,0:T(8,128)}, u32[]{:S(2)}) copy-start(f32[8,32]{1,0:T(8,128)} %param.19) | copy-start | bytes 3076
  419.0 96.8 %copy-start.13 = (f32[32]{0:T(128)S(1)}, f32[32]{0:T(128)}, u32[]{:S(2)}) copy-start(f32[32]{0:T(128)} %param.16) | copy-start | bytes 388
  419.0 97.3 %copy-start.6 = (f32[1,8,128,512]{3,1,2,0:T(8,128)S(1)}, f32[1,8,128,512]{3,1,2,0:T(8,128)}, u32[]{:S(2)}) copy-start(f32[1,8,128,512]{3,1,2,0:T(8,128)} %copy.30) | copy-start | bytes 6291460
  535.9 2.6 copy-start.1
Sparse Core Ops, SparseCore 0:
  11.5 214.9 all-gather.1
where the time goes:
time: 546 us; the launch traced here: 545 us
  waiting for transfers between devices  278 us (51%)
  other arithmetic  91.6 us (17%)
  blocking collectives  60.4 us (11%)
  local copies, waits for them, and re-layouts  49.4 us (9%)
  starting transfers between devices  28.5 us (5%)
  matrix products  22.4 us (4%)
  between operations  15 us (3%)
    ppermute x4, waiting for transfers between devices, padded_2(): lax.ppermute(lax.slice_in_dim(block, 0, width, axis=dim), axis, backward)  219 us
    add x3, other arithmetic, shards(): (1.0 - OMEGA) * head_field + OMEGA * (forcing + gathered) / diagonal  69.3 us
    ppermute x4, waiting for transfers between devices, padded_2(): lax.ppermute(lax.slice_in_dim(block, block.shape[dim] - width, None, axis...  58.8 us
    all_gather x1, blocking collectives, shards(): every_obs = lax.all_gather(observed, 'ens', axis=0, tiled=True)  25.5 us
    ppermute x4, starting transfers between devices, padded_2(): lax.ppermute(lax.slice_in_dim(block, block.shape[dim] - width, None, axis...  23 us
    dot_general x1, matrix products, shards(): lax.dot_general(mixing, piece_field, (((0,), (0,)), ((), ())), precision=...  19.6 us
    psum x1, blocking collectives, shards(): observed = lax.psum(picked, 'space')  18.1 us
    add x1, local copies, waits for them, and re-layouts, shards(): (1.0 - OMEGA) * head_field + OMEGA * (forcing + gathered) / diagonal  18 us
  transfers between devices with their start and end apart: 9, of which 7 were waited for; matrix products, arithmetic and copies ran while one was open for 25% of the time, Pallas kernels for 0%

commit v1 on v0

--- a/solution.py
+++ b/solution.py
@@ -94,8 +94,11 @@
     factor_lower = jnp.linalg.cholesky(system)
     gain_rows = solve_pair(factor_lower, obs_values[None, :] + perturb - observed)
     flat = log_perm.reshape(members, cell_count)
-    piece_field = lax.all_gather(flat, "ens", axis=0, tiled=True)
-    piece_dev = lax.all_gather(deviation, "ens", axis=0, tiled=True)
+    piece_field, piece_dev = jnp.split(
+        lax.all_gather(jnp.concatenate([flat, deviation], axis=1), "ens", axis=0, tiled=True),
+        [flat.shape[1]],
+        axis=1,
+    )
     mixing = jnp.dot(piece_dev, gain_rows.T, precision=HIGHEST)
     change = lax.dot_general(mixing, piece_field, (((0,), (0,)), ((), ())), precision=HIGHEST)
     updated = (flat + change / (total_members - 1)).reshape(log_perm.shape)

time: 546 us -> 566 us (1.037)
  waiting for transfers between devices: 278 us -> 296 us
  starting transfers between devices: 28.5 us -> 45.8 us
  blocking collectives: 60.4 us -> 43.8 us
    all_gather x1, waiting for transfers between devices: 0.01 us -> 159 us  [shards(): lax.all_gather(jnp.concatenate([flat, deviation], axis=1), 'ens', axis=0,...]
    ppermute x4, waiting for transfers between devices: 219 us -> 97 us  [padded_2(): lax.ppermute(lax.slice_in_dim(block, 0, width, axis=dim), axis, backward)]
    ppermute x4, waiting for transfers between devices: 58.8 us -> 39.7 us  [padded_2(): lax.ppermute(lax.slice_in_dim(block, block.shape[dim] - width, None, axis...]
    ppermute x4, starting transfers between devices: 23 us -> 40.3 us  [padded_2(): lax.ppermute(lax.slice_in_dim(block, block.shape[dim] - width, None, axis...]
    all_gather x1 -> x0, blocking collectives: 16.7 us -> none  [shards(): piece_dev = lax.all_gather(deviation, 'ens', axis=0, tiled=True)]
  transfers between devices with their start and end apart: 9 -> 9, of which waited for: 7 -> 8; matrix products, arithmetic and copies ran while one was open for 25% -> 4% of each run, Pallas kernels for 0% -> 0%
where the time goes in v1:
time: 566 us; the launch traced here: 565 us
  waiting for transfers between devices  296 us (52%)
  other arithmetic  93.2 us (16%)
  local copies, waits for them, and re-layouts  47.7 us (8%)
  starting transfers between devices  45.8 us (8%)
  blocking collectives  43.8 us (8%)
  matrix products  23.4 us (4%)
  between operations  15 us (3%)
    all_gather x1, waiting for transfers between devices, shards(): lax.all_gather(jnp.concatenate([flat, deviation], axis=1), 'ens', axis=0,...  159 us
    ppermute x4, waiting for transfers between devices, padded_2(): lax.ppermute(lax.slice_in_dim(block, 0, width, axis=dim), axis, backward)  97 us
    add x3, other arithmetic, shards(): (1.0 - OMEGA) * head_field + OMEGA * (forcing + gathered) / diagonal  69.4 us
    ppermute x4, starting transfers between devices, padded_2(): lax.ppermute(lax.slice_in_dim(block, block.shape[dim] - width, None, axis...  40.3 us
    ppermute x4, waiting for transfers between devices, padded_2(): lax.ppermute(lax.slice_in_dim(block, block.shape[dim] - width, None, axis...  39.7 us
    all_gather x1, blocking collectives, shards(): every_obs = lax.all_gather(observed, 'ens', axis=0, tiled=True)  26.4 us
    dot_general x1, matrix products, shards(): lax.dot_general(mixing, piece_field, (((0,), (0,)), ((), ())), precision=...  19.6 us
    add x1, local copies, waits for them, and re-layouts, shards(): (1.0 - OMEGA) * head_field + OMEGA * (forcing + gathered) / diagonal  18 us
  transfers between devices with their start and end apart: 9, of which 8 were waited for; matrix products, arithmetic and copies ran while one was open for 4% of the time, Pallas kernels for 0%

profile of v1, /device:TPU:1, one launch (start us, length us, event | category | flops | bytes accessed | tf_op | source)
XLA Modules:
  0.0 564.7 jit_solution(7277823546648534783)
XLA Ops:
  7.2 2.0 exp.3
  10.8 5.7 %collective-permute-start = (f32[8,1,64,512]{3,2,1,0:T(8,128)}, f32[8,1,64,512]{3,2,1,0:T(8,128)S(1)}, u32[]{:S(2)}, u32[]{:S(2)}) collective-permute-start(f32[8,1,64,512]{3,2,1,0:T(8,128)} %get-tuple-element.10), channel_id=1, source_target_pairs={{0,16},{16,32},{32,48},{48,64},{64,80},{80,96},{96,112},{1,17},{17... | collective-permute-start | bytes 3145736 | tf_op jit(solution)/shard_map/ppermute | solution.py:19
  21.4 7.1 %collective-permute-start.2 = (f32[8,1,64,512]{3,2,1,0:T(8,128)}, f32[8,1,64,512]{3,2,1,0:T(8,128)}, u32[]{:S(2)}, u32[]{:S(2)}) collective-permute-start(f32[8,1,64,512]{3,2,1,0:T(8,128)} %broadcast_in_dim.53), channel_id=1, source_target_pairs={{0,16},{16,32},{32,48},{48,64},{64,80},{80,96},{96,112},{1,17},{17... | collective-permute-start | bytes 3145736 | tf_op jit(solution)/shard_map/ppermute | solution.py:19
  28.5 2.1 fusion.5
  32.3 1.8 broadcast_multiply_fusion
  34.2 4.3 collective-permute-done
  38.5 24.8 %collective-permute-done.1 = f32[8,1,64,512]{3,2,1,0:T(8,128)} collective-permute-done((f32[8,1,64,512]{3,2,1,0:T(8,128)}, f32[8,1,64,512]{3,2,1,0:T(8,128)}, u32[]{:S(2)}, u32[]{:S(2)}) %collective-permute-start.1) | collective-permute-done | bytes 1048608 | tf_op jit(solution)/shard_map/ppermute | solution.py:22
  63.3 3.7 select_maximum_fusion.6
  67.0 18.8 %collective-permute-done.3 = f32[8,1,64,512]{3,2,1,0:T(8,128)} collective-permute-done((f32[8,1,64,512]{3,2,1,0:T(8,128)}, f32[8,1,64,512]{3,2,1,0:T(8,128)}, u32[]{:S(2)}, u32[]{:S(2)}) %collective-permute-start.3) | collective-permute-done | bytes 1048608 | tf_op jit(solution)/shard_map/ppermute | solution.py:22
  86.1 4.7 select_maximum_fusion.4
  90.8 23.9 %fusion.72 = f32[8,2,64,512]{3,2,1,0:T(8,128)} fusion(f32[8,4,66,514]{3,2,1,0:T(8,128)S(1)} %select_maximum_fusion.4, f32[8,1,64,512]{3,2,1,0:T(8,128)} %collective-permute-done.3, f32[8,2,64,512]{3,2,1,0:T(8,128)} %copy-done.5, f32[8,1,64,512]{3,2,1,0:T(8,128)} %collective-permute-done.2, f32[2,64,512]{2,1,0:T(8,128)S(1)} %copy-done.7, ...), kind=kLoop, calls=%fused_computation.141 | loop fusion | flops 87031808 | bytes 114032640 | tf_op jit(solution)/shard_map/add | solution.py:78
  114.7 1.9 fusion.122
  116.6 23.7 %collective-permute-start.4 = (f32[8,1,64,512]{3,2,1,0:T(8,128)S(1)}, f32[8,1,64,512]{3,2,1,0:T(8,128)S(1)}, u32[]{:S(2)}, u32[]{:S(2)}) collective-permute-start(f32[8,1,64,512]{3,2,1,0:T(8,128)S(1)} %get-tuple-element.8), channel_id=1, source_target_pairs={{0,16},{16,32},{32,48},{48,64},{64,80},{80,96},{96,112},{1,17},{17... | collective-permute-start | bytes 3145736 | tf_op jit(solution)/shard_map/ppermute | solution.py:19
  141.8 19.3 %collective-permute-done.4 = f32[8,1,64,512]{3,2,1,0:T(8,128)S(1)} collective-permute-done((f32[8,1,64,512]{3,2,1,0:T(8,128)S(1)}, f32[8,1,64,512]{3,2,1,0:T(8,128)S(1)}, u32[]{:S(2)}, u32[]{:S(2)}) %collective-permute-start.4) | collective-permute-done | bytes 1048608 | tf_op jit(solution)/shard_map/ppermute | solution.py:19
  161.1 27.8 %collective-permute-done.5 = f32[8,1,64,512]{3,2,1,0:T(8,128)S(1)} collective-permute-done((f32[8,1,64,512]{3,2,1,0:T(8,128)S(1)}, f32[8,1,64,512]{3,2,1,0:T(8,128)S(1)}, u32[]{:S(2)}, u32[]{:S(2)}) %collective-permute-start.5) | collective-permute-done | bytes 1048608 | tf_op jit(solution)/shard_map/ppermute | solution.py:22
  189.9 2.7 select_maximum_fusion.2
  192.6 22.7 %fusion.41 = f32[8,2,64,512]{3,2,1,0:T(8,128)} fusion(f32[8,4,66,514]{3,2,1,0:T(8,128)S(1)} %select_maximum_fusion.2, f32[8,1,64,512]{3,2,1,0:T(8,128)} %copy-done.9, f32[8,2,64,512]{3,2,1,0:T(8,128)} %fusion.72, f32[8,1,64,512]{3,2,1,0:T(8,128)S(1)} %collective-permute-done.4, f32[2,64,512]{2,1,0:T(8,128)S(1)} %copy-done.7, ...), kind=kLoop, calls=%fused_computation.84 | loop fusion | flops 87556096 | bytes 113770496 | tf_op jit(solution)/shard_map/add | solution.py:78
  217.1 3.8 collective-permute-start.6
  222.2 2.5 copy.18
  224.7 16.0 %collective-permute-done.6 = f32[8,1,64,512]{3,2,1,0:T(8,128)S(1)} collective-permute-done((f32[8,1,64,512]{3,2,1,0:T(8,128)S(1)}, f32[8,1,64,512]{3,2,1,0:T(8,128)S(1)}, u32[]{:S(2)}, u32[]{:S(2)}) %collective-permute-start.6) | collective-permute-done | bytes 1048608 | tf_op jit(solution)/shard_map/ppermute | solution.py:19
  240.8 25.7 %collective-permute-done.7 = f32[8,1,64,512]{3,2,1,0:T(8,128)S(1)} collective-permute-done((f32[8,1,64,512]{3,2,1,0:T(8,128)S(1)}, f32[8,1,64,512]{3,2,1,0:T(8,128)S(1)}, u32[]{:S(2)}, u32[]{:S(2)}) %collective-permute-start.7) | collective-permute-done | bytes 1048608 | tf_op jit(solution)/shard_map/ppermute | solution.py:22
  267.4 2.7 select_maximum_fusion
  270.1 22.8 %fusion.10 = f32[8,2,64,512]{3,2,1,0:T(8,128)} fusion(f32[8,4,66,514]{3,2,1,0:T(8,128)S(1)} %select_maximum_fusion, f32[8,1,64,512]{3,2,1,0:T(8,128)} %copy-done.8, f32[8,2,64,512]{3,2,1,0:T(8,128)} %fusion.41, f32[8,1,64,512]{3,2,1,0:T(8,128)S(1)} %collective-permute-done.6, f32[2,64,512]{2,1,0:T(8,128)S(1)} %copy-done.7, ...), kind=kLoop, calls=%fused_computation.27 | loop fusion | flops 87556096 | bytes 113770496 | tf_op jit(solution)/shard_map/add | solution.py:78
  292.9 18.0 %copy.12 = f32[8,2,64,512]{0,3,2,1:T(8,128)} copy(f32[8,2,64,512]{3,2,1,0:T(8,128)} %fusion.10) | data formatting | bytes 4194304 | tf_op jit(solution)/shard_map/add | solution.py:78
  310.9 11.1 %gather_fusion = f32[32,8]{1,0:T(8,128)S(1)} fusion(f32[8,65536]{0,1:T(8,128)} %bitcast.34, s32[1024]{0:T(1024)S(1)} %pad_clamp_fusion), kind=kCustom, calls=%fused_computation | custom fusion | bytes 2176 | tf_op jit(solution)/shard_map/jit(_take)/gather | solution.py:82
  322.1 17.4 %psum.7 = f32[8,32]{1,0:T(8,128)S(1)} all-reduce(f32[8,32]{1,0:T(8,128)S(1)} %multiply_bitcast_fusion), channel_id=1, replica_groups=mesh['space'=8,'ens'=16] {'space'}, use_global_device_ids=true, to_apply=%region_0.1 | all-reduce | flops 256 | bytes 2048 | tf_op jit(solution)/shard_map/psum | solution.py:87
  339.5 26.4 %all_gather.6 = f32[128,32]{1,0:T(8,128)S(1)} all-gather(f32[8,32]{1,0:T(8,128)S(1)} %psum.7), channel_id=1, replica_groups=mesh['space'=8,'ens'=16] {'ens'}, dimensions={0}, use_global_device_ids=true | all-gather | bytes 17408 | tf_op jit(solution)/shard_map/all_gather | solution.py:88
  368.5 2.9 cholesky.16
  372.8 2.4 custom-call.8
  375.6 159.0 %all-gather.2.cloned.1.call-done = f32[128,65568]{1,0:T(8,128)} async-done(((f32[8,65568]{1,0:T(8,128)}), f32[128,65568]{1,0:T(8,128)}) %all-gather.2.cloned.1.call-update) | async-done | bytes 33570832 | tf_op jit(solution)/shard_map/all_gather | solution.py:98
  535.7 19.6 %fusion = f32[8,65536]{1,0:T(8,128)S(1)} fusion(f32[8,65536]{1,0:T(8,128)S(1)} %bitcast.36, f32[128,8]{1,0:T(8,128)S(1)} %fusion.106, f32[128,65568]{1,0:T(8,128)} %all-gather.2.cloned.1.call-done), kind=kOutput, calls=%fused_computation.2 | convolution fusion | flops 806354944 | bytes 37752832 | tf_op jit(solution)/shard_map/dot_general | solution.py:103
  555.3 2.5 copy.16
  (67 shorter events, 19.7 us)
Async XLA Ops:
  7.2 21.4 %copy-start = (f32[16]{0:T(128)S(1)}, f32[16]{0:T(128)}, u32[]{:S(2)}) copy-start(f32[16]{0:T(128)} %param.14) | copy-start | bytes 196
  7.2 527.5 %all-gather.2.cloned.1.call-start = ((), (), s32[]{:S(2)}) async-start(), calls=%async_computation | async-start | bytes 35721216 | tf_op jit(solution)/shard_map/all_gather | solution.py:98
  9.2 8.7 %copy-start.10 = (f32[2,64,512]{2,1,0:T(8,128)S(1)}, f32[2,64,512]{2,1,0:T(8,128)}, u32[]{:S(2)}) copy-start(f32[2,64,512]{2,1,0:T(8,128)} %param.12) | copy-start | bytes 786436
  10.8 17.8 %copy-start.15 = (s32[16]{0:T(128)S(1)}, s32[16]{0:T(128)}, u32[]{:S(2)}) copy-start(s32[16]{0:T(128)} %param.13) | copy-start | bytes 196
  10.8 27.7 %collective-permute-start = (f32[8,1,64,512]{3,2,1,0:T(8,128)}, f32[8,1,64,512]{3,2,1,0:T(8,128)S(1)}, u32[]{:S(2)}, u32[]{:S(2)}) collective-permute-start(f32[8,1,64,512]{3,2,1,0:T(8,128)} %get-tuple-element.10), channel_id=1, source_target_pairs={{0,16},{16,32},{32,48},{48,64},{64,80},{80,96},{96,112},{1,17},{17... | collective-permute-start | bytes 3145736 | tf_op jit(solution)/shard_map/ppermute | solution.py:19
  16.4 15.9 %copy-start.7 = (f32[2,64,512]{2,1,0:T(8,128)S(1)}, f32[2,64,512]{2,1,0:T(8,128)}, u32[]{:S(2)}) copy-start(f32[2,64,512]{2,1,0:T(8,128)} %param.11) | copy-start | bytes 786436
  16.5 46.8 %collective-permute-start.1 = (f32[8,1,64,512]{3,2,1,0:T(8,128)}, f32[8,1,64,512]{3,2,1,0:T(8,128)}, u32[]{:S(2)}, u32[]{:S(2)}) collective-permute-start(f32[8,1,64,512]{3,2,1,0:T(8,128)} %get-tuple-element.11), channel_id=1, source_target_pairs={{16,0},{32,16},{48,32},{64,48},{80,64},{96,80},{112,96},{17,1},{33... | collective-permute-start | bytes 3145736 | tf_op jit(solution)/shard_map/ppermute | solution.py:22
  19.0 66.7 %collective-permute-start.3 = (f32[8,1,64,512]{3,2,1,0:T(8,128)}, f32[8,1,64,512]{3,2,1,0:T(8,128)}, u32[]{:S(2)}, u32[]{:S(2)}) collective-permute-start(f32[8,1,64,512]{3,2,1,0:T(8,128)} %broadcast_in_dim.55), channel_id=1, source_target_pairs={{16,0},{32,16},{48,32},{64,48},{80,64},{96,80},{112,96},{17,1},{33... | collective-permute-start | bytes 3145736 | tf_op jit(solution)/shard_map/ppermute | solution.py:22
  21.4 64.3 %collective-permute-start.2 = (f32[8,1,64,512]{3,2,1,0:T(8,128)}, f32[8,1,64,512]{3,2,1,0:T(8,128)}, u32[]{:S(2)}, u32[]{:S(2)}) collective-permute-start(f32[8,1,64,512]{3,2,1,0:T(8,128)} %broadcast_in_dim.53), channel_id=1, source_target_pairs={{0,16},{16,32},{32,48},{48,64},{64,80},{80,96},{96,112},{1,17},{17... | collective-permute-start | bytes 3145736 | tf_op jit(solution)/shard_map/ppermute | solution.py:19
  34.2 51.6 %copy-start.11 = (f32[2,64,512]{2,1,0:T(8,128)S(1)}, f32[2,64,512]{2,1,0:T(8,128)}, u32[]{:S(2)}) copy-start(f32[2,64,512]{2,1,0:T(8,128)} %param.12) | copy-start | bytes 786436
  86.0 4.7 copy-start.5
  86.0 4.7 copy-start.2
  114.7 75.2 %copy-start.4 = (f32[8,2,64,512]{3,2,1,0:T(8,128)S(1)}, f32[8,2,64,512]{3,2,1,0:T(8,128)}, u32[]{:S(2)}) copy-start(f32[8,2,64,512]{3,2,1,0:T(8,128)} %fusion.72) | copy-start | bytes 6291460
  116.6 44.5 %collective-permute-start.4 = (f32[8,1,64,512]{3,2,1,0:T(8,128)S(1)}, f32[8,1,64,512]{3,2,1,0:T(8,128)S(1)}, u32[]{:S(2)}, u32[]{:S(2)}) collective-permute-start(f32[8,1,64,512]{3,2,1,0:T(8,128)S(1)} %get-tuple-element.8), channel_id=1, source_target_pairs={{0,16},{16,32},{32,48},{48,64},{64,80},{80,96},{96,112},{1,17},{17... | collective-permute-start | bytes 3145736 | tf_op jit(solution)/shard_map/ppermute | solution.py:19
  140.3 48.6 %collective-permute-start.5 = (f32[8,1,64,512]{3,2,1,0:T(8,128)S(1)}, f32[8,1,64,512]{3,2,1,0:T(8,128)S(1)}, u32[]{:S(2)}, u32[]{:S(2)}) collective-permute-start(f32[8,1,64,512]{3,2,1,0:T(8,128)S(1)} %get-tuple-element.9), channel_id=1, source_target_pairs={{16,0},{32,16},{48,32},{64,48},{80,64},{96,80},{112,96},{17,1},{33... | collective-permute-start | bytes 3145736 | tf_op jit(solution)/shard_map/ppermute | solution.py:22
  188.9 1.0 copy-start.9
  217.1 23.7 %collective-permute-start.6 = (f32[8,1,64,512]{3,2,1,0:T(8,128)S(1)}, f32[8,1,64,512]{3,2,1,0:T(8,128)S(1)}, u32[]{:S(2)}, u32[]{:S(2)}) collective-permute-start(f32[8,1,64,512]{3,2,1,0:T(8,128)S(1)} %get-tuple-element.6), channel_id=1, source_target_pairs={{0,16},{16,32},{32,48},{48,64},{64,80},{80,96},{96,112},{1,17},{17... | collective-permute-start | bytes 3145736 | tf_op jit(solution)/shard_map/ppermute | solution.py:19
  220.9 45.6 %collective-permute-start.7 = (f32[8,1,64,512]{3,2,1,0:T(8,128)S(1)}, f32[8,1,64,512]{3,2,1,0:T(8,128)S(1)}, u32[]{:S(2)}, u32[]{:S(2)}) collective-permute-start(f32[8,1,64,512]{3,2,1,0:T(8,128)S(1)} %get-tuple-element.7), channel_id=1, source_target_pairs={{16,0},{32,16},{48,32},{64,48},{80,64},{96,80},{112,96},{17,1},{33... | collective-permute-start | bytes 3145736 | tf_op jit(solution)/shard_map/ppermute | solution.py:22
  222.2 2.5 copy-start.13
  222.2 45.2 %copy-start.3 = (f32[8,2,64,512]{3,2,1,0:T(8,128)S(1)}, f32[8,2,64,512]{3,2,1,0:T(8,128)}, u32[]{:S(2)}) copy-start(f32[8,2,64,512]{3,2,1,0:T(8,128)} %fusion.41) | copy-start | bytes 6291460
  266.5 1.0 copy-start.8
  292.9 73.0 %copy-start.6 = (f32[1,8,128,512]{3,1,2,0:T(8,128)S(1)}, f32[1,8,128,512]{3,1,2,0:T(8,128)}, u32[]{:S(2)}) copy-start(f32[1,8,128,512]{3,1,2,0:T(8,128)} %copy.18) | copy-start | bytes 6291460
  367.4 0.7 copy-start.16
  367.4 7.8 %copy-start.12 = (f32[8,32]{1,0:T(8,128)S(1)}, f32[8,32]{1,0:T(8,128)}, u32[]{:S(2)}) copy-start(f32[8,32]{1,0:T(8,128)} %param.19) | copy-start | bytes 3076
  367.4 7.8 %copy-start.14 = (f32[32]{0:T(128)S(1)}, f32[32]{0:T(128)}, u32[]{:S(2)}) copy-start(f32[32]{0:T(128)} %param.16) | copy-start | bytes 388
  555.3 2.6 copy-start.1
Sparse Core Ops, SparseCore 0:
  367.5 167.0 all-gather.1
